TPU v7x, 32 devices: a whole 2x2x4 slice. The times are simulated.
32 devices in a mesh: groups: 2 (over x), width: 8 (over z, y), guide: 2 (over core).
Axes of the slice: x: 2, y: 2, z: 4, core: 2. Of those that a mesh axis runs over, the one named last changes fastest.
Arguments:
- latent: float32 [16, 8, 2048], P(None, None, ('groups', 'width')), parts along dimension 2, may hold values from -6 to 6
- starts: int32 [16], P(('groups', 'width')), parts along dimension 0, may hold values from 0 to 1023, as said below
- counts: int32 [2048], P(('groups', 'width')), parts along dimension 0, may hold values from 1 to 3, as said below
- step_index: int32 [2], P('groups'), parts along dimension 0, may hold values from 0 to 27
- cond_mod: float32 [2, 3, 2432], P('guide'), may hold values from -3 to 3
- w_patch: bfloat16 [64, 2432], replicated, may hold values from -0.75 to 0.75
- w_qkv: bfloat16 [2432, 3840], P('width'), may hold values from -0.125 to 0.125
- w_out: bfloat16 [1280, 2432], replicated, may hold values from -0.15625 to 0.15625
- w_final: bfloat16 [2432, 64], replicated, may hold values from -0.125 to 0.125
- w_dec: bfloat16 [144, 512], replicated, may hold values from -0.5 to 0.5
Outputs:
- denoised: float32 [16, 8, 2048], P(None, 'guide', ('groups', 'width')), parts along dimension 2
- features: bfloat16 [8, 2048, 512], P('guide', ('groups', 'width')), parts along dimension 1
There are 2 independent parts, one for each index of `groups`. A program takes and returns all parts, laid end to end along the dimension named above; an argument that names none is the same for every part. Nothing has to cross between parts.
Inputs may be any that keep to these rules, and one draw needn't show every extreme that they name: window k starts between column k * 128 and column (k + 1) * 128 - 1 and covers 2 * 128 columns, wrapping around the panorama. `counts`: the number of windows whose columns, as given by starts, include the column.
All inputs are finite; a program needn't handle non-finite values.
Results may differ from a plain program's by a relative error of at most 0.013.
Values may be sent and summed in bfloat16 or wider, within the bound.
A program may use at most 128 MiB of HBM per device.

v0:
```python
import jax
import jax.numpy as jnp
from jax import lax
from jax.sharding import PartitionSpec as P

HEAD = 64
STEPS = 28
guidance = 4.0
epsilon = 1e-06


def from_behind(x, axis, by):
    peers = lax.axis_size(axis)
    return lax.ppermute(x, axis, [(i, (i + by) % peers) for i in range(peers)])


def from_partner(block, axis, stride):
    count = lax.axis_size(axis)
    route = []
    for low in range(count):
        high = low | 1 << stride
        if high != low and high < count:
            route += [(low, high), (high, low)]
    return lax.ppermute(block, axis, route)


def extended(block, sides, width):
    for axis, dim in sides:
        count = lax.axis_size(axis)
        forward = [(i, i + 1) for i in range(count - 1)]
        backward = [(target, source) for source, target in forward]
        low = lax.ppermute(
            lax.slice_in_dim(block, block.shape[dim] - width, None, axis=dim), axis, forward
        )
        high = lax.ppermute(lax.slice_in_dim(block, 0, width, axis=dim), axis, backward)
        block = jnp.concatenate([low, block, high], axis=dim)
    return block


def layer_norm(values):
    centered = values - jnp.mean(values, axis=-1, keepdims=True)
    spread = jnp.mean(centered * centered, axis=-1, keepdims=True)
    return centered * lax.rsqrt(spread + epsilon)


def head_norm(values):
    return values * lax.rsqrt(jnp.mean(values * values, axis=-1, keepdims=True) + epsilon)


def patchify(window):
    channels, height, breadth = window.shape
    folded = window.reshape(channels, height // 2, 2, breadth // 2, 2).transpose(1, 3, 2, 4, 0)
    return folded.reshape(height // 2 * (breadth // 2), 4 * channels)


def unpatchify(tokens, channels, height, breadth):
    folded = tokens.reshape(height // 2, breadth // 2, 2, 2, channels).transpose(4, 0, 2, 1, 3)
    return folded.reshape(channels, height, breadth)


def attend(queries, key_rows, value_rows):
    scores = jnp.einsum("bqhe,bkhe->bhqk", queries, key_rows, preferred_element_type=jnp.float32)
    scores = scores / jnp.sqrt(jnp.float32(queries.shape[-1]))
    weights = jax.nn.softmax(scores, axis=-1).astype(jnp.bfloat16)
    mixed = jnp.einsum("bhqk,bkhe->bqhe", weights, value_rows, preferred_element_type=jnp.float32)
    return mixed.astype(jnp.bfloat16)


def convolve(padded, w_dec):
    channels = padded.shape[0]
    height = padded.shape[1] - 2
    breadth = padded.shape[2] - 2
    shifted = [
        padded[:, row_at : row_at + height, col_at : col_at + breadth]
        for row_at in range(3)
        for col_at in range(3)
    ]
    stacked = jnp.stack(shifted).reshape(9 * channels, height * breadth)
    summed = lax.dot_general(
        stacked, w_dec, (((0,), (0,)), ((), ())), preferred_element_type=jnp.float32
    )
    return jax.nn.silu(summed).astype(jnp.bfloat16).reshape(height, breadth, w_dec.shape[1])


def halves(values):
    high = lax.reduce_precision(values, 8, 7)
    return (high.astype(jnp.bfloat16), (values - high).astype(jnp.bfloat16))


def fold(modulation, w_patch, w_qkv, place):
    patch = w_patch.astype(jnp.float32)
    patch = patch - jnp.mean(patch, axis=1, keepdims=True)
    rows = jnp.concatenate([patch * (1.0 + modulation[1]), modulation[0:1]], axis=0)
    depth = w_qkv.shape[0]
    rows = lax.dynamic_slice_in_dim(rows, place * depth, depth, 1)
    high, low = halves(rows)
    both = jnp.dot(jnp.concatenate([high, low], axis=0), w_qkv, preferred_element_type=jnp.float32)
    return both[: rows.shape[0]] + both[rows.shape[0] :]


def fetch_next(block):
    return from_behind(block, "width", -1)


def pass_right(block):
    return from_behind(block.astype(jnp.bfloat16), "width", 1).astype(block.dtype)


def shards(latent, starts, counts, step_index, cond_mod, w_patch, w_qkv, w_out, w_final, w_dec):
    guide_at = lax.axis_index("guide")
    place = lax.axis_index("width")
    channels, height, columns = latent.shape
    half_rows = height // 2
    fraction = (step_index[0].astype(jnp.float32) + 1.0) / STEPS
    sigma = 3.0 * fraction / (1.0 + 2.0 * fraction)
    modulation = cond_mod[0]
    own_cols = latent.astype(jnp.bfloat16)
    ahead = fetch_next(own_cols)
    further = fetch_next(ahead)
    three_blocks = jnp.concatenate([own_cols, ahead, further], axis=2)
    offset = starts[0] - place * columns
    window = lax.dynamic_slice_in_dim(three_blocks, offset, 2 * columns, 2)
    patches = patchify(window)
    token_count = patches.shape[0]
    hidden = jnp.dot(patches, w_patch, preferred_element_type=jnp.float32)
    centered = hidden - jnp.mean(hidden, axis=-1, keepdims=True)
    rstd = lax.rsqrt(jnp.mean(centered * centered, axis=-1, keepdims=True) + epsilon)
    heads = w_qkv.shape[1] // (3 * HEAD)
    folded = lax.psum(fold(modulation, w_patch, w_qkv, place), "width")
    patch_rows = w_patch.shape[0]
    high, low = halves(folded[:patch_rows])
    projected = jnp.dot(
        jnp.concatenate([patches, patches], axis=1),
        jnp.concatenate([high, low], axis=0),
        preferred_element_type=jnp.float32,
    )
    projected = projected * rstd + folded[patch_rows : patch_rows + 1]
    projected = projected.reshape(token_count, 3, heads, HEAD)
    queries = head_norm(projected[:, 0]).astype(jnp.bfloat16)
    key_rows = head_norm(projected[:, 1]).astype(jnp.bfloat16)
    value_rows = projected[:, 2].astype(jnp.bfloat16)
    attended = attend(queries[None], key_rows[None], value_rows[None])[0]
    attended = attended.reshape(token_count, heads * HEAD)
    mixed_out = jnp.dot(attended, w_out, preferred_element_type=jnp.float32)
    residual = hidden + modulation[2] * mixed_out
    final_in = layer_norm(residual).astype(jnp.bfloat16)
    result = jnp.dot(final_in, w_final, preferred_element_type=jnp.float32)
    velocity_win = unpatchify(result, channels, height, 2 * columns)
    branch_pair = lax.all_to_all(
        velocity_win[None].astype(jnp.bfloat16), "guide", split_axis=2, concat_axis=0, tiled=True
    ).astype(jnp.float32)
    guided = branch_pair[1] + guidance * (branch_pair[0] - branch_pair[1])
    spread_out = jnp.zeros((channels, half_rows, 3 * columns), jnp.float32)
    spread_out = lax.dynamic_update_slice_in_dim(spread_out, guided, offset, 2)
    carried = pass_right(spread_out[:, :, 2 * columns :])
    arrived = pass_right(spread_out[:, :, columns : 2 * columns] + carried)
    summed = spread_out[:, :, :columns] + arrived
    velocity = summed / counts.astype(jnp.float32)[None, None, :]
    mine_rows = lax.dynamic_slice_in_dim(latent, guide_at * half_rows, half_rows, 1)
    denoised = mine_rows - sigma * velocity
    padded = extended(denoised.astype(jnp.bfloat16), (("guide", 1), ("width", 2)), 1)
    features = convolve(padded, w_dec)
    return (denoised, features)


def solution(mesh):
    return jax.shard_map(
        shards,
        mesh=mesh,
        in_specs=(
            P(None, None, ("groups", "width")),
            P(("groups", "width")),
            P(("groups", "width")),
            P("groups"),
            P("guide", None, None),
            P(),
            P("width", None),
            P(),
            P(),
            P(),
        ),
        out_specs=(P(None, "guide", ("groups", "width")), P("guide", ("groups", "width"), None)),
        check_vma=False,
    )
```

profile of v0, /device:TPU:0, one launch (start us, length us, event | category | flops | bytes accessed | tf_op | source)
XLA Modules:
  0.0 190.0 jit_solution(14800418378556094931)
XLA Ops:
  7.2 1.0 convert_element_type.102
  8.2 6.0 %collective-permute-start = (bf16[16,8,128]{2,1,0:T(8,128)(2,1)S(1)}, bf16[16,8,128]{2,1,0:T(8,128)(2,1)S(1)}, u32[]{:S(2)}, u32[]{:S(2)}) collective-permute-start(bf16[16,8,128]{2,1,0:T(8,128)(2,1)S(1)} %convert_element_type.102), channel_id=1, source_target_pairs={{0,14},{2,0},{4,2},{6,4},{8,6},{10,8},{12,10},{14,12},{1,15},{3,1}... | collective-permute-start | bytes 98312 | tf_op jit(solution)/shard_map/ppermute | solution.py:14
  14.3 0.8 slice_reduce_fusion.1
  15.0 1.1 convert_reduce_fusion
  16.2 1.1 fusion.20
  17.3 0.1 reduce-precision_convert_fusion.1
  17.4 0.7 fusion.29
  18.1 2.7 %collective-permute-start.1 = (bf16[16,8,128]{2,1,0:T(8,128)(2,1)S(1)}, bf16[16,8,128]{2,1,0:T(8,128)(2,1)S(1)}, u32[]{:S(2)}, u32[]{:S(2)}) collective-permute-start(bf16[16,8,128]{2,1,0:T(8,128)(2,1)S(1)} %collective-permute-done), channel_id=1, source_target_pairs={{0,14},{2,0},{4,2},{6,4},{8,6},{10,8},{12,10},{14,12},{1,15},{3,1}... | collective-permute-start | bytes 98312 | tf_op jit(solution)/shard_map/ppermute | solution.py:14
  20.9 1.2 slice_add_fusion
  22.7 0.1 fusion.34
  22.9 0.3 copy.24
  23.1 0.4 copy.25
  23.6 0.9 fusion.51
  24.5 2.2 %copy-done.1 = f32[512,2432]{1,0:T(8,128)} copy-done((f32[512,2432]{1,0:T(8,128)}, f32[512,2432]{1,0:T(8,128)S(1)}, u32[]{:S(2)}) %copy-start.1) | copy-done | bytes 4980760
  26.7 0.6 multiply_reduce_fusion.2
  27.3 71.3 %all-reduce.2.cloned.1.call-done = f32[65,3840]{1,0:T(8,128)} async-done(((f32[65,3840]{1,0:T(8,128)}), f32[65,3840]{1,0:T(8,128)}) %all-reduce.2.cloned.1.call-update) | async-done | bytes 998416 | tf_op jit(solution)/shard_map/psum | solution.py:129
  98.6 1.3 reduce-precision_convert_fusion
  99.9 0.9 slice_reduce_fusion
  100.9 4.3 %multiply_add_fusion = f32[512,3840]{1,0:T(8,128)} fusion(f32[3840]{0:T(1024)S(1)} %slice_reduce_fusion, f32[512]{0:T(512)S(1)} %add_rsqrt_fusion.3, bf16[64,3840]{1,0:T(8,128)(2,1)S(1)} %get-tuple-element.9, bf16[64,3840]{1,0:T(8,128)(2,1)S(1)} %get-tuple-element.8, bf16[512,64]{0,1:T(8,128)(2,1)S(1)} %bitcast.139), kind=kOutput, calls=%fused_computation.7 | convolution fusion | flops 509476864 | bytes 8930304 | tf_op jit(solution)/shard_map/dot_general | solution.py:132
  105.2 9.1 %copy.26 = f32[512,3840]{0,1:T(8,128)} copy(f32[512,3840]{1,0:T(8,128)} %multiply_add_fusion) | data formatting | bytes 15728640 | tf_op jit(solution)/shard_map/add | solution.py:137
  114.2 3.3 %multiply_reduce_fusion.3 = (f32[512,20]{0,1:T(8,128)S(1)}, f32[512,20]{0,1:T(8,128)S(1)}) fusion(f32[512,3,20,64]{0,3,2,1:T(8,128)} %bitcast.131), kind=kLoop, calls=%fused_computation.18 | loop fusion | flops 2600960 | bytes 5324800 | tf_op jit(solution)/shard_map/reduce_sum | solution.py:47
  117.6 12.8 %fusion.52 = (f32[20,512]{1,0:T(8,128)S(1)}, f32[20,512,512]{1,2,0:T(8,128)}) fusion(f32[512,3,20,64]{0,3,2,1:T(8,128)} %bitcast.132, f32[512,20]{0,1:T(8,128)S(1)} %get-tuple-element.26, f32[512,20]{0,1:T(8,128)S(1)} %get-tuple-element.25), kind=kOutput, calls=%fused_computation.118 | convolution fusion | flops 689439232 | bytes 26337280 | tf_op jit(solution)/shard_map/sub | solution.py:64
  130.4 9.9 %fusion.12 = bf16[20,64,512]{2,1,0:T(8,128)(2,1)S(1)} fusion(f32[20,512,512]{1,2,0:T(8,128)} %get-tuple-element.22, f32[20,512]{1,0:T(8,128)S(1)} %get-tuple-element.21, f32[512,3,20,64]{0,3,2,1:T(8,128)} %bitcast.133), kind=kOutput, calls=%fused_computation.24 | convolution fusion | flops 682229760 | bytes 23633920 | tf_op jit(solution)/shard_map/bhqk,bkhe->bqhe/dot_general | solution.py:65
  140.3 6.3 %fusion.53 = (f32[512]{0:T(512)S(1)}, f32[512,2432]{1,0:T(8,128)S(1)}) fusion(f32[512,2432]{1,0:T(8,128)S(1)} %bitcast.130, bf16[512,1280]{0,1:T(8,128)(2,1)S(1)} %bitcast.136, bf16[1280,2432]{1,0:T(8,128)(2,1)} %param.17, f32[2432]{0:T(1024)S(1)} %get-tuple-element.4), kind=kOutput, calls=%fused_computation.119 | convolution fusion | flops 3191406080 | bytes 17509888 | tf_op jit(solution)/shard_map/dot_general | solution.py:144
  146.6 0.6 multiply_reduce_fusion.1
  147.3 0.3 copy-done.3
  147.6 1.1 fusion.15
  148.7 0.4 copy.28
  149.2 0.2 copy.29
  149.3 3.8 %all_to_all.4 = bf16[1,16,8,256]{3,1,0,2:T(8,128)(2,1)S(1)} all-to-all(bf16[1,16,8,256]{3,1,0,2:T(8,128)(2,1)S(1)} %copy.29), channel_id=1, replica_groups=mesh['groups'=2,'width'=8,'guide'=2] {'guide'}, dimensions={2} | all-to-all | bytes 131072 | tf_op jit(solution)/shard_map/all_to_all | solution.py:149
  153.3 2.6 %dynamic_update_slice.3 = f32[16,4,384]{2,1,0:T(4,128)S(1)} dynamic-update-slice(f32[16,4,384]{2,1,0:T(4,128)S(1)} %broadcast_in_dim.2, f32[16,4,256]{2,1,0:T(4,128)S(1)} %copy.32, s32[]{:T(128)} %constant.20.clone.1, s32[]{:T(128)} %constant.20.clone.1, s32[]{:T(128)S(6)} %select_n.11) | dynamic-update-slice | bytes 131076 | tf_op jit(solution)/shard_map/dynamic_update_slice | solution.py:154
  155.9 1.4 collective-permute-start.2
  157.2 5.1 %collective-permute-done.2 = bf16[16,4,128]{2,1,0:T(4,128)(2,1)S(1)} collective-permute-done((bf16[16,4,128]{2,1,0:T(4,128)(2,1)S(1)}, bf16[16,4,128]{2,1,0:T(4,128)(2,1)S(1)}, u32[]{:S(2)}, u32[]{:S(2)}) %collective-permute-start.2) | collective-permute-done | bytes 16416 | tf_op jit(solution)/shard_map/ppermute | solution.py:14
  163.2 5.7 %collective-permute-done.3 = bf16[16,4,128]{2,1,0:T(4,128)(2,1)S(1)} collective-permute-done((bf16[16,4,128]{2,1,0:T(4,128)(2,1)S(1)}, bf16[16,4,128]{2,1,0:T(4,128)(2,1)S(1)}, u32[]{:S(2)}, u32[]{:S(2)}) %collective-permute-start.3) | collective-permute-done | bytes 16416 | tf_op jit(solution)/shard_map/ppermute | solution.py:14
  168.9 0.6 fusion.48
  169.5 1.3 collective-permute-start.4
  170.8 1.3 collective-permute-start.5
  172.1 1.8 collective-permute-done.5
  174.0 1.3 collective-permute-start.6
  175.3 1.3 collective-permute-start.7
  176.6 0.3 collective-permute-done.6
  177.0 4.1 %collective-permute-done.7 = bf16[16,6,1]{2,1,0:T(8,128)(2,1)S(1)} collective-permute-done((bf16[16,6,1]{2,1,0:T(8,128)(2,1)S(1)}, bf16[16,6,1]{2,1,0:T(8,128)(2,1)S(1)}, u32[]{:S(2)}, u32[]{:S(2)}) %collective-permute-start.7) | collective-permute-done | bytes 224 | tf_op jit(solution)/shard_map/ppermute | solution.py:35
  181.1 0.1 constant_dynamic-update-slice_fusion.6
  181.2 0.1 constant_dynamic-update-slice_fusion.5
  181.4 0.1 constant_dynamic-update-slice_fusion.3
  181.5 0.1 constant_dynamic-update-slice_fusion.2
  181.7 0.1 constant_dynamic-update-slice_fusion
  181.8 1.3 multiply_convert_fusion.6
  (45 shorter events, 0.7 us)
Async XLA Ops:
  7.2 10.3 %copy-start = (bf16[304,3840]{1,0:T(8,128)(2,1)S(1)}, bf16[304,3840]{1,0:T(8,128)(2,1)}, u32[]{:S(2)}) copy-start(bf16[304,3840]{1,0:T(8,128)(2,1)} %param.16) | copy-start | bytes 7004164
  7.2 91.4 %all-reduce.2.cloned.1.call-start = ((), (), s32[]{:S(2)}) async-start(), calls=%async_computation.1 | async-start | bytes 2211840 | tf_op jit(solution)/shard_map/psum | solution.py:129
  8.2 9.9 %collective-permute-start = (bf16[16,8,128]{2,1,0:T(8,128)(2,1)S(1)}, bf16[16,8,128]{2,1,0:T(8,128)(2,1)S(1)}, u32[]{:S(2)}, u32[]{:S(2)}) collective-permute-start(bf16[16,8,128]{2,1,0:T(8,128)(2,1)S(1)} %convert_element_type.102), channel_id=1, source_target_pairs={{0,14},{2,0},{4,2},{6,4},{8,6},{10,8},{12,10},{14,12},{1,15},{3,1}... | collective-permute-start | bytes 98312 | tf_op jit(solution)/shard_map/ppermute | solution.py:14
  17.4 6.1 %copy-start.2 = (bf16[64,2432]{1,0:T(8,128)(2,1)S(1)}, bf16[64,2432]{1,0:T(8,128)(2,1)}, u32[]{:S(2)}) copy-start(bf16[64,2432]{1,0:T(8,128)(2,1)} %param.15) | copy-start | bytes 933892
  18.1 4.6 %collective-permute-start.1 = (bf16[16,8,128]{2,1,0:T(8,128)(2,1)S(1)}, bf16[16,8,128]{2,1,0:T(8,128)(2,1)S(1)}, u32[]{:S(2)}, u32[]{:S(2)}) collective-permute-start(bf16[16,8,128]{2,1,0:T(8,128)(2,1)S(1)} %collective-permute-done), channel_id=1, source_target_pairs={{0,14},{2,0},{4,2},{6,4},{8,6},{10,8},{12,10},{14,12},{1,15},{3,1}... | collective-permute-start | bytes 98312 | tf_op jit(solution)/shard_map/ppermute | solution.py:14
  24.5 2.2 %copy-start.1 = (f32[512,2432]{1,0:T(8,128)}, f32[512,2432]{1,0:T(8,128)S(1)}, u32[]{:S(2)}) copy-start(f32[512,2432]{1,0:T(8,128)S(1)} %get-tuple-element.20) | copy-start | bytes 14942212
  117.6 22.7 %slice-start = ((s8[4980736]{0:T(1024)(128)(4,1)}), s8[786432]{0:T(1024)(128)(4,1)S(1)}, s32[]{:S(2)}) async-start(s8[4980736]{0:T(1024)(128)(4,1)} %bitcast.129), calls=%async_computation.2 | async-start | bytes 1572864
  130.4 9.9 %slice-start.1 = ((s8[4980736]{0:T(1024)(128)(4,1)}), s8[4194304]{0:T(1024)(128)(4,1)S(1)}, s32[]{:S(2)}) async-start(s8[4980736]{0:T(1024)(128)(4,1)} %bitcast.129), calls=%async_computation.3 | async-start | bytes 8388608
  146.6 1.0 copy-start.3
  147.3 15.8 %copy-start.6 = (s32[128]{0:T(128)S(1)}, s32[128]{0:T(128)}, u32[]{:S(2)}) copy-start(s32[128]{0:T(128)} %param.12) | copy-start | bytes 1540
  147.3 21.6 %copy-start.4 = (f32[16,8,128]{2,1,0:T(8,128)S(1)}, f32[16,8,128]{2,1,0:T(8,128)}, u32[]{:S(2)}) copy-start(f32[16,8,128]{2,1,0:T(8,128)} %param.10) | copy-start | bytes 196612
  147.3 34.5 %copy-start.5 = (bf16[144,512]{1,0:T(8,128)(2,1)S(1)}, bf16[144,512]{1,0:T(8,128)(2,1)}, u32[]{:S(2)}) copy-start(bf16[144,512]{1,0:T(8,128)(2,1)} %param.19) | copy-start | bytes 442372
  155.9 6.5 %collective-permute-start.2 = (bf16[16,4,128]{2,1,0:T(4,128)(2,1)S(1)}, bf16[16,4,128]{2,1,0:T(4,128)(2,1)S(1)}, u32[]{:S(2)}, u32[]{:S(2)}) collective-permute-start(bf16[16,4,128]{2,1,0:T(4,128)(2,1)S(1)} %slice.194), channel_id=1, source_target_pairs={{0,2},{2,4},{4,6},{6,8},{8,10},{10,12},{12,14},{14,0},{1,3},{3,5},... | collective-permute-start | bytes 49160 | tf_op jit(solution)/shard_map/ppermute | solution.py:14
  162.4 6.5 %collective-permute-start.3 = (bf16[16,4,128]{2,1,0:T(4,128)(2,1)S(1)}, bf16[16,4,128]{2,1,0:T(4,128)(2,1)S(1)}, u32[]{:S(2)}, u32[]{:S(2)}) collective-permute-start(bf16[16,4,128]{2,1,0:T(4,128)(2,1)S(1)} %fusion.38), channel_id=1, source_target_pairs={{0,2},{2,4},{4,6},{6,8},{8,10},{10,12},{12,14},{14,0},{1,3},{3,5},... | collective-permute-start | bytes 49160 | tf_op jit(solution)/shard_map/ppermute | solution.py:14
  169.5 2.6 %collective-permute-start.4 = (bf16[16,1,128]{2,1,0:T(2,128)(2,1)S(1)}, bf16[16,1,128]{2,1,0:T(2,128)(2,1)S(1)}, u32[]{:S(2)}, u32[]{:S(2)}) collective-permute-start(bf16[16,1,128]{2,1,0:T(2,128)(2,1)S(1)} %get-tuple-element.17), channel_id=1, source_target_pairs={{0,1},{2,3},{4,5},{6,7},{8,9},{10,11},{12,13},{14,15},{16,17},{18,... | collective-permute-start | bytes 12296 | tf_op jit(solution)/shard_map/ppermute | solution.py:32
  170.8 3.1 %collective-permute-start.5 = (bf16[16,1,128]{2,1,0:T(2,128)(2,1)S(1)}, bf16[16,1,128]{2,1,0:T(2,128)(2,1)S(1)}, u32[]{:S(2)}, u32[]{:S(2)}) collective-permute-start(bf16[16,1,128]{2,1,0:T(2,128)(2,1)S(1)} %get-tuple-element.18), channel_id=1, source_target_pairs={{1,0},{3,2},{5,4},{7,6},{9,8},{11,10},{13,12},{15,14},{17,16},{19,... | collective-permute-start | bytes 12296 | tf_op jit(solution)/shard_map/ppermute | solution.py:35
  174.0 2.9 %collective-permute-start.6 = (bf16[16,6,1]{2,1,0:T(8,128)(2,1)S(1)}, bf16[16,6,1]{2,1,0:T(8,128)(2,1)S(1)}, u32[]{:S(2)}, u32[]{:S(2)}) collective-permute-start(bf16[16,6,1]{2,1,0:T(8,128)(2,1)S(1)} %get-tuple-element.15), channel_id=1, source_target_pairs={{0,2},{2,4},{4,6},{6,8},{8,10},{10,12},{12,14},{1,3},{3,5},{5,7},{... | collective-permute-start | bytes 584 | tf_op jit(solution)/shard_map/ppermute | solution.py:32
  175.3 5.8 %collective-permute-start.7 = (bf16[16,6,1]{2,1,0:T(8,128)(2,1)S(1)}, bf16[16,6,1]{2,1,0:T(8,128)(2,1)S(1)}, u32[]{:S(2)}, u32[]{:S(2)}) collective-permute-start(bf16[16,6,1]{2,1,0:T(8,128)(2,1)S(1)} %get-tuple-element.14), channel_id=1, source_target_pairs={{2,0},{4,2},{6,4},{8,6},{10,8},{12,10},{14,12},{3,1},{5,3},{7,5},{... | collective-permute-start | bytes 584 | tf_op jit(solution)/shard_map/ppermute | solution.py:35
Sparse Core Ops, SparseCore 0:
  22.2 76.3 all-reduce.1
where the time goes:
time: 191 us; the launch traced here: 190 us
  waiting for transfers between devices  88.3 us (46%)
  matrix products  37.3 us (20%)
  local copies, waits for them, and re-layouts  16.5 us (9%)
  between operations  15.8 us (8%)
  starting transfers between devices  15.4 us (8%)
  other arithmetic  12.9 us (7%)
  blocking collectives  3.79 us (2%)
    psum x1, waiting for transfers between devices, shards(): folded = lax.psum(fold(modulation, w_patch, w_qkv, place), 'width')  71.3 us
    sub x1, matrix products, attend(): weights = jax.nn.softmax(scores, axis=-1).astype(jnp.bfloat16)  12.8 us
    ppermute x4, waiting for transfers between devices, from_behind(): return lax.ppermute(x, axis, [(i, (i + by) % peers) for i in range(peers)])  10.8 us
    ppermute x4, starting transfers between devices, from_behind(): return lax.ppermute(x, axis, [(i, (i + by) % peers) for i in range(peers)])  10.2 us
    dot_general x1, matrix products, attend(): jnp.einsum('bhqk,bkhe->bqhe', weights, value_rows, preferred_element_type...  9.86 us
    add x1, local copies, waits for them, and re-layouts, shards(): projected = projected * rstd + folded[patch_rows:patch_rows + 1]  9.07 us
    dot_general x1, matrix products, shards(): mixed_out = jnp.dot(attended, w_out, preferred_element_type=jnp.float32)  6.33 us
    ppermute x2, waiting for transfers between devices, extended(): lax.ppermute(lax.slice_in_dim(block, 0, width, axis=dim), axis, backward)  5.84 us
  transfers between devices with their start and end apart: 9, of which 6 were waited for; matrix products, arithmetic and copies ran while one was open for 4% of the time, Pallas kernels for 0%

commit v1 on v0

--- a/solution.py
+++ b/solution.py
@@ -7,6 +7,12 @@
 STEPS = 28
 guidance = 4.0
 epsilon = 1e-06
+
+
+def add_all(x, axis):
+    parts = lax.all_gather(x, axis, axis=0, tiled=False)
+    acc = parts.sum(axis=0)
+    return acc
 
 
 def from_behind(x, axis, by):
@@ -126,7 +132,7 @@
     centered = hidden - jnp.mean(hidden, axis=-1, keepdims=True)
     rstd = lax.rsqrt(jnp.mean(centered * centered, axis=-1, keepdims=True) + epsilon)
     heads = w_qkv.shape[1] // (3 * HEAD)
-    folded = lax.psum(fold(modulation, w_patch, w_qkv, place), "width")
+    folded = add_all(fold(modulation, w_patch, w_qkv, place), "width")
     patch_rows = w_patch.shape[0]
     high, low = halves(folded[:patch_rows])
     projected = jnp.dot(

time: 191 us -> 239 us (1.25)
  waiting for transfers between devices: 88.3 us -> 134 us
    all_gather x0 -> x1, waiting for transfers between devices: none -> 113 us  [add_all(): parts = lax.all_gather(x, axis, axis=0, tiled=False)]
    psum x1 -> x0, waiting for transfers between devices: 71.3 us -> none  [shards(): folded = lax.psum(fold(modulation, w_patch, w_qkv, place), 'width')]
    reduce_sum x0 -> x1, other arithmetic: none -> 4.07 us  [add_all(): acc = parts.sum(axis=0)]
    ppermute x4, waiting for transfers between devices: 10.8 us -> 14.7 us  [from_behind(): return lax.ppermute(x, axis, [(i, (i + by) % peers) for i in range(peers)])]
  transfers between devices with their start and end apart: 9 -> 9, of which waited for: 6 -> 8; matrix products, arithmetic and copies ran while one was open for 4% -> 1% of each run, Pallas kernels for 0% -> 0%
where the time goes in v1:
time: 239 us
  waiting for transfers between devices  134 us (56%)
  matrix products  37.2 us (16%)
  starting transfers between devices  17 us (7%)
  between operations  15.8 us (7%)
  local copies, waits for them, and re-layouts  15.7 us (7%)
  other arithmetic  14.9 us (6%)
  blocking collectives  3.79 us (2%)
    all_gather x1, waiting for transfers between devices, add_all(): parts = lax.all_gather(x, axis, axis=0, tiled=False)  113 us
    ppermute x4, waiting for transfers between devices, from_behind(): return lax.ppermute(x, axis, [(i, (i + by) % peers) for i in range(peers)])  14.7 us
    sub x1, matrix products, attend(): weights = jax.nn.softmax(scores, axis=-1).astype(jnp.bfloat16)  12.7 us
    ppermute x4, starting transfers between devices, from_behind(): return lax.ppermute(x, axis, [(i, (i + by) % peers) for i in range(peers)])  11.8 us
    dot_general x1, matrix products, attend(): jnp.einsum('bhqk,bkhe->bqhe', weights, value_rows, preferred_element_type...  9.84 us
    add x1, local copies, waits for them, and re-layouts, shards(): projected = projected * rstd + folded[patch_rows:patch_rows + 1]  9.07 us
    dot_general x1, matrix products, shards(): mixed_out = jnp.dot(attended, w_out, preferred_element_type=jnp.float32)  6.33 us
    ppermute x2, waiting for transfers between devices, extended(): lax.ppermute(lax.slice_in_dim(block, 0, width, axis=dim), axis, backward)  5.67 us
  transfers between devices with their start and end apart: 9, of which 8 were waited for; matrix products, arithmetic and copies ran while one was open for 1% of the time, Pallas kernels for 0%

profile of v1, /device:TPU:0, one launch (start us, length us, event | category | flops | bytes accessed | tf_op | source)
XLA Modules:
  0.0 238.7 jit_solution(14106973194773137940)
XLA Ops:
  7.2 0.9 slice_reduce_fusion.1
  8.2 1.1 convert_reduce_fusion
  9.3 1.1 fusion.21
  10.4 0.1 reduce-precision_convert_fusion.1
  10.6 0.7 fusion.30
  11.3 1.2 fusion.16
  12.5 6.1 %collective-permute-start = (bf16[16,8,128]{2,1,0:T(8,128)(2,1)S(1)}, bf16[16,8,128]{2,1,0:T(8,128)(2,1)S(1)}, u32[]{:S(2)}, u32[]{:S(2)}) collective-permute-start(bf16[16,8,128]{2,1,0:T(8,128)(2,1)S(1)} %convert_element_type.102), channel_id=1, source_target_pairs={{0,14},{2,0},{4,2},{6,4},{8,6},{10,8},{12,10},{14,12},{1,15},{3,1}... | collective-permute-start | bytes 98312 | tf_op jit(solution)/shard_map/ppermute | solution.py:20
  18.6 1.6 collective-permute-done
  20.2 5.0 %collective-permute-start.1 = (bf16[16,8,128]{2,1,0:T(8,128)(2,1)S(1)}, bf16[16,8,128]{2,1,0:T(8,128)(2,1)S(1)}, u32[]{:S(2)}, u32[]{:S(2)}) collective-permute-start(bf16[16,8,128]{2,1,0:T(8,128)(2,1)S(1)} %collective-permute-done), channel_id=1, source_target_pairs={{0,14},{2,0},{4,2},{6,4},{8,6},{10,8},{12,10},{14,12},{1,15},{3,1}... | collective-permute-start | bytes 98312 | tf_op jit(solution)/shard_map/ppermute | solution.py:20
  25.9 1.5 collective-permute-done.1
  27.4 0.1 fusion.35
  27.5 0.3 copy.24
  27.8 0.4 copy.25
  28.2 0.9 fusion.52
  29.2 2.2 copy-done.2
  31.3 0.6 multiply_reduce_fusion.2
  32.0 113.4 %all-gather.4.cloned.1.call-done = f32[8,65,3840]{2,1,0:T(8,128)} async-done(((f32[1,65,3840]{2,1,0:T(8,128)}), f32[8,65,3840]{2,1,0:T(8,128)}) %all-gather.4.cloned.1.call-update) | async-done | bytes 7987216 | tf_op jit(solution)/shard_map/all_gather | solution.py:13
  145.4 4.1 %reduce_sum.82 = f32[65,3840]{1,0:T(8,128)S(1)} reduce(f32[8,65,3840]{2,1,0:T(8,128)} %all-gather.4.cloned.1.call-done, f32[]{:T(128)} %constant.19.clone.1), dimensions={0}, to_apply=%region_1.0 | reduce | flops 1747200 | bytes 8985604 | tf_op jit(solution)/shard_map/reduce_sum | solution.py:14
  149.6 4.3 %multiply_add_fusion = f32[512,3840]{1,0:T(8,128)} fusion(f32[3840]{0:T(1024)S(1)} %slice_reduce_fusion, f32[512]{0:T(512)S(1)} %add_rsqrt_fusion.3, bf16[64,3840]{1,0:T(8,128)(2,1)S(1)} %get-tuple-element.9, bf16[64,3840]{1,0:T(8,128)(2,1)S(1)} %get-tuple-element.8, bf16[512,64]{0,1:T(8,128)(2,1)S(1)} %bitcast.141), kind=kOutput, calls=%fused_computation.7 | convolution fusion | flops 509476864 | bytes 8930304 | tf_op jit(solution)/shard_map/dot_general | solution.py:138
  153.9 9.1 %copy.26 = f32[512,3840]{0,1:T(8,128)} copy(f32[512,3840]{1,0:T(8,128)} %multiply_add_fusion) | data formatting | bytes 15728640 | tf_op jit(solution)/shard_map/add | solution.py:143
  163.0 3.3 %multiply_reduce_fusion.3 = (f32[512,20]{0,1:T(8,128)S(1)}, f32[512,20]{0,1:T(8,128)S(1)}) fusion(f32[512,3,20,64]{0,3,2,1:T(8,128)} %bitcast.133), kind=kLoop, calls=%fused_computation.18 | loop fusion | flops 2600960 | bytes 5324800 | tf_op jit(solution)/shard_map/reduce_sum | solution.py:53
  166.4 12.7 %fusion.53 = (f32[20,512]{1,0:T(8,128)S(1)}, f32[20,512,512]{1,2,0:T(8,128)}) fusion(f32[512,3,20,64]{0,3,2,1:T(8,128)} %bitcast.134, f32[512,20]{0,1:T(8,128)S(1)} %get-tuple-element.26, f32[512,20]{0,1:T(8,128)S(1)} %get-tuple-element.25), kind=kOutput, calls=%fused_computation.119 | convolution fusion | flops 689439232 | bytes 26337280 | tf_op jit(solution)/shard_map/sub | solution.py:70
  179.1 9.8 %fusion.12 = bf16[20,64,512]{2,1,0:T(8,128)(2,1)S(1)} fusion(f32[20,512,512]{1,2,0:T(8,128)} %get-tuple-element.22, f32[20,512]{1,0:T(8,128)S(1)} %get-tuple-element.21, f32[512,3,20,64]{0,3,2,1:T(8,128)} %bitcast.135), kind=kOutput, calls=%fused_computation.24 | convolution fusion | flops 682229760 | bytes 23633920 | tf_op jit(solution)/shard_map/bhqk,bkhe->bqhe/dot_general | solution.py:71
  189.0 6.3 %fusion.54 = (f32[512]{0:T(512)S(1)}, f32[512,2432]{1,0:T(8,128)S(1)}) fusion(f32[512,2432]{1,0:T(8,128)S(1)} %bitcast.132, bf16[512,1280]{0,1:T(8,128)(2,1)S(1)} %bitcast.138, bf16[1280,2432]{1,0:T(8,128)(2,1)} %param.17, f32[2432]{0:T(1024)S(1)} %get-tuple-element.4), kind=kOutput, calls=%fused_computation.120 | convolution fusion | flops 3191406080 | bytes 17509888 | tf_op jit(solution)/shard_map/dot_general | solution.py:150
  195.3 0.6 multiply_reduce_fusion.1
  196.0 0.3 copy-done.4
  196.3 1.1 fusion.15
  197.4 0.4 copy.28
  197.9 0.2 copy.29
  198.1 3.8 %all_to_all.4 = bf16[1,16,8,256]{3,1,0,2:T(8,128)(2,1)S(1)} all-to-all(bf16[1,16,8,256]{3,1,0,2:T(8,128)(2,1)S(1)} %copy.29), channel_id=1, replica_groups=mesh['groups'=2,'width'=8,'guide'=2] {'guide'}, dimensions={2} | all-to-all | bytes 131072 | tf_op jit(solution)/shard_map/all_to_all | solution.py:155
  202.0 2.6 %dynamic_update_slice.3 = f32[16,4,384]{2,1,0:T(4,128)S(1)} dynamic-update-slice(f32[16,4,384]{2,1,0:T(4,128)S(1)} %broadcast_in_dim.2, f32[16,4,256]{2,1,0:T(4,128)S(1)} %copy.32, s32[]{:T(128)} %constant.20.clone.1, s32[]{:T(128)} %constant.20.clone.1, s32[]{:T(128)S(6)} %select_n.11) | dynamic-update-slice | bytes 131076 | tf_op jit(solution)/shard_map/dynamic_update_slice | solution.py:160
  204.6 0.6 collective-permute-start.2
  205.2 5.9 %collective-permute-done.2 = bf16[16,4,128]{2,1,0:T(4,128)(2,1)S(1)} collective-permute-done((bf16[16,4,128]{2,1,0:T(4,128)(2,1)S(1)}, bf16[16,4,128]{2,1,0:T(4,128)(2,1)S(1)}, u32[]{:S(2)}, u32[]{:S(2)}) %collective-permute-start.2) | collective-permute-done | bytes 16416 | tf_op jit(solution)/shard_map/ppermute | solution.py:20
  211.9 5.7 %collective-permute-done.3 = bf16[16,4,128]{2,1,0:T(4,128)(2,1)S(1)} collective-permute-done((bf16[16,4,128]{2,1,0:T(4,128)(2,1)S(1)}, bf16[16,4,128]{2,1,0:T(4,128)(2,1)S(1)}, u32[]{:S(2)}, u32[]{:S(2)}) %collective-permute-start.3) | collective-permute-done | bytes 16416 | tf_op jit(solution)/shard_map/ppermute | solution.py:20
  217.6 0.6 fusion.49
  218.2 1.3 collective-permute-start.4
  219.5 1.3 collective-permute-start.5
  220.8 1.8 collective-permute-done.5
  222.7 1.3 collective-permute-start.6
  224.0 1.3 collective-permute-start.7
  225.3 0.4 collective-permute-done.6
  225.9 3.9 %collective-permute-done.7 = bf16[16,6,1]{2,1,0:T(8,128)(2,1)S(1)} collective-permute-done((bf16[16,6,1]{2,1,0:T(8,128)(2,1)S(1)}, bf16[16,6,1]{2,1,0:T(8,128)(2,1)S(1)}, u32[]{:S(2)}, u32[]{:S(2)}) %collective-permute-start.7) | collective-permute-done | bytes 224 | tf_op jit(solution)/shard_map/ppermute | solution.py:41
  229.8 0.1 constant_dynamic-update-slice_fusion.6
  229.9 0.1 constant_dynamic-update-slice_fusion.5
  230.1 0.1 constant_dynamic-update-slice_fusion.3
  230.2 0.1 constant_dynamic-update-slice_fusion.2
  230.4 0.1 constant_dynamic-update-slice_fusion
  230.5 1.3 multiply_convert_fusion.6
  (48 shorter events, 0.8 us)
Async XLA Ops:
  7.2 3.4 %copy-start = (bf16[304,3840]{1,0:T(8,128)(2,1)S(1)}, bf16[304,3840]{1,0:T(8,128)(2,1)}, u32[]{:S(2)}) copy-start(bf16[304,3840]{1,0:T(8,128)(2,1)} %param.16) | copy-start | bytes 7004164
  7.2 138.2 %all-gather.4.cloned.1.call-start = ((), (), s32[]{:S(2)}) async-start(), calls=%async_computation.1 | async-start | bytes 9953280 | tf_op jit(solution)/shard_map/all_gather | solution.py:13
  10.4 2.1 copy-start.5
  10.6 17.6 %copy-start.3 = (bf16[64,2432]{1,0:T(8,128)(2,1)S(1)}, bf16[64,2432]{1,0:T(8,128)(2,1)}, u32[]{:S(2)}) copy-start(bf16[64,2432]{1,0:T(8,128)(2,1)} %param.15) | copy-start | bytes 933892
  12.5 7.7 %collective-permute-start = (bf16[16,8,128]{2,1,0:T(8,128)(2,1)S(1)}, bf16[16,8,128]{2,1,0:T(8,128)(2,1)S(1)}, u32[]{:S(2)}, u32[]{:S(2)}) collective-permute-start(bf16[16,8,128]{2,1,0:T(8,128)(2,1)S(1)} %convert_element_type.102), channel_id=1, source_target_pairs={{0,14},{2,0},{4,2},{6,4},{8,6},{10,8},{12,10},{14,12},{1,15},{3,1}... | collective-permute-start | bytes 98312 | tf_op jit(solution)/shard_map/ppermute | solution.py:20
  20.2 7.2 %collective-permute-start.1 = (bf16[16,8,128]{2,1,0:T(8,128)(2,1)S(1)}, bf16[16,8,128]{2,1,0:T(8,128)(2,1)S(1)}, u32[]{:S(2)}, u32[]{:S(2)}) collective-permute-start(bf16[16,8,128]{2,1,0:T(8,128)(2,1)S(1)} %collective-permute-done), channel_id=1, source_target_pairs={{0,14},{2,0},{4,2},{6,4},{8,6},{10,8},{12,10},{14,12},{1,15},{3,1}... | collective-permute-start | bytes 98312 | tf_op jit(solution)/shard_map/ppermute | solution.py:20
  29.1 2.2 copy-start.2
  166.4 22.6 %slice-start = ((s8[4980736]{0:T(1024)(128)(4,1)}), s8[786432]{0:T(1024)(128)(4,1)S(1)}, s32[]{:S(2)}) async-start(s8[4980736]{0:T(1024)(128)(4,1)} %bitcast.131), calls=%async_computation.2 | async-start | bytes 1572864
  179.1 9.9 %slice-start.1 = ((s8[4980736]{0:T(1024)(128)(4,1)}), s8[4194304]{0:T(1024)(128)(4,1)S(1)}, s32[]{:S(2)}) async-start(s8[4980736]{0:T(1024)(128)(4,1)} %bitcast.131), calls=%async_computation.3 | async-start | bytes 8388608
  195.3 1.0 copy-start.4
  196.0 15.8 %copy-start.7 = (s32[128]{0:T(128)S(1)}, s32[128]{0:T(128)}, u32[]{:S(2)}) copy-start(s32[128]{0:T(128)} %param.12) | copy-start | bytes 1540
  196.0 34.5 %copy-start.6 = (bf16[144,512]{1,0:T(8,128)(2,1)S(1)}, bf16[144,512]{1,0:T(8,128)(2,1)}, u32[]{:S(2)}) copy-start(bf16[144,512]{1,0:T(8,128)(2,1)} %param.19) | copy-start | bytes 442372
  196.3 35.5 %copy-start.1 = (bf16[304,3840]{1,0:T(8,128)(2,1)S(1)}, bf16[304,3840]{1,0:T(8,128)(2,1)}, u32[]{:S(2)}) copy-start(bf16[304,3840]{1,0:T(8,128)(2,1)} %param.16) | copy-start | bytes 7004164
  204.6 6.5 %collective-permute-start.2 = (bf16[16,4,128]{2,1,0:T(4,128)(2,1)S(1)}, bf16[16,4,128]{2,1,0:T(4,128)(2,1)S(1)}, u32[]{:S(2)}, u32[]{:S(2)}) collective-permute-start(bf16[16,4,128]{2,1,0:T(4,128)(2,1)S(1)} %slice.196), channel_id=1, source_target_pairs={{0,2},{2,4},{4,6},{6,8},{8,10},{10,12},{12,14},{14,0},{1,3},{3,5},... | collective-permute-start | bytes 49160 | tf_op jit(solution)/shard_map/ppermute | solution.py:20
  211.1 6.5 %collective-permute-start.3 = (bf16[16,4,128]{2,1,0:T(4,128)(2,1)S(1)}, bf16[16,4,128]{2,1,0:T(4,128)(2,1)S(1)}, u32[]{:S(2)}, u32[]{:S(2)}) collective-permute-start(bf16[16,4,128]{2,1,0:T(4,128)(2,1)S(1)} %fusion.39), channel_id=1, source_target_pairs={{0,2},{2,4},{4,6},{6,8},{8,10},{10,12},{12,14},{14,0},{1,3},{3,5},... | collective-permute-start | bytes 49160 | tf_op jit(solution)/shard_map/ppermute | solution.py:20
  218.2 2.6 %collective-permute-start.4 = (bf16[16,1,128]{2,1,0:T(2,128)(2,1)S(1)}, bf16[16,1,128]{2,1,0:T(2,128)(2,1)S(1)}, u32[]{:S(2)}, u32[]{:S(2)}) collective-permute-start(bf16[16,1,128]{2,1,0:T(2,128)(2,1)S(1)} %get-tuple-element.17), channel_id=1, source_target_pairs={{0,1},{2,3},{4,5},{6,7},{8,9},{10,11},{12,13},{14,15},{16,17},{18,... | collective-permute-start | bytes 12296 | tf_op jit(solution)/shard_map/ppermute | solution.py:38
  219.5 3.1 %collective-permute-start.5 = (bf16[16,1,128]{2,1,0:T(2,128)(2,1)S(1)}, bf16[16,1,128]{2,1,0:T(2,128)(2,1)S(1)}, u32[]{:S(2)}, u32[]{:S(2)}) collective-permute-start(bf16[16,1,128]{2,1,0:T(2,128)(2,1)S(1)} %get-tuple-element.18), channel_id=1, source_target_pairs={{1,0},{3,2},{5,4},{7,6},{9,8},{11,10},{13,12},{15,14},{17,16},{19,... | collective-permute-start | bytes 12296 | tf_op jit(solution)/shard_map/ppermute | solution.py:41
  222.7 3.0 %collective-permute-start.6 = (bf16[16,6,1]{2,1,0:T(8,128)(2,1)S(1)}, bf16[16,6,1]{2,1,0:T(8,128)(2,1)S(1)}, u32[]{:S(2)}, u32[]{:S(2)}) collective-permute-start(bf16[16,6,1]{2,1,0:T(8,128)(2,1)S(1)} %get-tuple-element.15), channel_id=1, source_target_pairs={{0,2},{2,4},{4,6},{6,8},{8,10},{10,12},{12,14},{1,3},{3,5},{5,7},{... | collective-permute-start | bytes 584 | tf_op jit(solution)/shard_map/ppermute | solution.py:38
  224.0 5.8 %collective-permute-start.7 = (bf16[16,6,1]{2,1,0:T(8,128)(2,1)S(1)}, bf16[16,6,1]{2,1,0:T(8,128)(2,1)S(1)}, u32[]{:S(2)}, u32[]{:S(2)}) collective-permute-start(bf16[16,6,1]{2,1,0:T(8,128)(2,1)S(1)} %get-tuple-element.14), channel_id=1, source_target_pairs={{2,0},{4,2},{6,4},{8,6},{10,8},{12,10},{14,12},{3,1},{5,3},{7,5},{... | collective-permute-start | bytes 584 | tf_op jit(solution)/shard_map/ppermute | solution.py:41
Sparse Core Ops, SparseCore 0:
  12.6 132.7 all-gather.3
